TPU v7x, 512 devices: a whole 4x8x8 slice. The times are simulated.
512 devices in a mesh: pts: 128 (over x, z, y_lo, core), lmk: 4 (over y_hi).
Axes of the slice: x: 4, y: 8 (y_hi: 4, y_lo: 2; y = y_hi * 2 + y_lo), z: 8, core: 2. Of those that a mesh axis runs over, the one named last changes fastest.
Arguments:
- points: bfloat16 [32768, 768], P('pts'), may hold values from -6 to 6
- landmarks: bfloat16 [384, 768], P('lmk'), may hold values from -6 to 6
- panels: bfloat16 [128, 384, 2048], P('pts', None, 'lmk'), may hold values from -0.3125 to 0.3125
- panel_index: int32 [1], replicated, may hold values from 0 to 127
- assignment: int32 [32768], P('pts'), may hold values from 0 to 4095, as said below
Outputs:
- centroid_sums: float32 [4096, 2048], P('pts', 'lmk')
- cluster_counts: int32 [4096], P('pts')
Inputs may be any that keep to these rules, and one draw needn't show every extreme that they name: `assignment`: owner of a cluster c is c // 32. In each aligned block of 256 points (the points of one device) at most 4 points have clusters of one owner; one owner, the same for every block, has exactly 4 points in every block.
All inputs are finite; a program needn't handle non-finite values.
Results may differ from a plain program's by a relative error of at most 0.0017.
Values may be sent and summed in bfloat16 or wider, within the bound.
A program may use at most 64 MiB of HBM per device.

v0:
```python
import math
import jax
import jax.numpy as jnp
from jax import lax
from jax.sharding import PartitionSpec as P

CLUSTERS = 4096


def spread(block, axis, holder):
    block = jnp.where(lax.axis_index(axis) == holder, block, jnp.zeros_like(block))
    return lax.psum(block, axis)


def unit_rows(values_in):
    widened = values_in.astype(jnp.float32)
    scale = lax.rsqrt(jnp.mean(widened * widened, axis=1, keepdims=True) + 1e-06)
    return (widened * scale).astype(jnp.bfloat16)


def kernel_rows(unit_points, unit_marks):
    scores = lax.dot_general(
        unit_points, unit_marks, (((1,), (1,)), ((), ())), preferred_element_type=jnp.float32
    )
    return jnp.exp(scores * (0.5 / math.sqrt(unit_points.shape[1]))).astype(jnp.bfloat16)


def body(points, landmarks, panels, panel_index, assignment):
    point_groups = lax.axis_size("pts")
    point_rows = points.shape[0]
    unit_points = unit_rows(points)
    kernel = kernel_rows(
        unit_points, unit_rows(lax.all_gather(landmarks, "lmk", axis=0, tiled=True))
    )
    factor_panel = spread(panels[0], "pts", panel_index[0])
    owned_clusters = CLUSTERS // point_groups
    capacity = 2 * point_rows // point_groups
    owners = assignment // owned_clusters
    local_id = assignment - owners * owned_clusters
    owner_hits = (owners[:, None] == jnp.arange(point_groups, dtype=jnp.int32)[None, :]).astype(
        jnp.int32
    )
    slot_rank = jnp.sum(jnp.cumsum(owner_hits, axis=0) * owner_hits, axis=1) - 1
    slot_ids = jnp.full((point_groups, capacity), -1, jnp.int32).at[owners, slot_rank].set(local_id)
    features = jnp.dot(kernel, factor_panel, preferred_element_type=jnp.float32).astype(
        jnp.bfloat16
    )
    slots = (
        jnp.zeros((point_groups, capacity, features.shape[1]), jnp.bfloat16)
        .at[owners, slot_rank]
        .set(features)
    )
    arrived, arrived_ids = (
        lax.all_to_all(slots, "pts", split_axis=0, concat_axis=0, tiled=True),
        lax.all_to_all(slot_ids, "pts", split_axis=0, concat_axis=0, tiled=True),
    )
    received = arrived.reshape(-1, arrived.shape[2])
    membership = (
        arrived_ids.reshape(-1)[None, :] == jnp.arange(owned_clusters, dtype=jnp.int32)[:, None]
    )
    totals = jnp.dot(membership.astype(jnp.bfloat16), received, preferred_element_type=jnp.float32)
    counts = jnp.sum(membership.astype(jnp.int32), axis=1)
    mean_count = point_rows * point_groups / CLUSTERS
    return (totals / mean_count, counts)


def solution(mesh):
    in_specs = (P("pts", None), P("lmk", None), P("pts", None, "lmk"), P(), P("pts"))
    out_specs = (P("pts", "lmk"), P("pts"))
    return jax.shard_map(body, mesh=mesh, in_specs=in_specs, out_specs=out_specs, check_vma=False)
```

profile of v0, /device:TPU:1, one launch (start us, length us, event | category | flops | bytes accessed | tf_op | source)
XLA Modules:
  0.0 1064.7 jit_solution(14033932260171003460)
XLA Ops:
  7.2 0.0 all-reduce.2.cloned.1.call-start
  7.9 0.8 select_bitcast_fusion
  8.7 0.0 all-reduce.2.cloned.1.call-update
  8.7 0.1 copy.13
  8.8 0.2 fusion.15
  9.1 0.2 fusion.16
  9.4 11.1 %scatter_fusion = s32[128,4]{0,1:T(4,128)S(1)} fusion(s32[128,4]{0,1:T(4,128)S(1)} %broadcast_in_dim.8, s32[256]{0:T(256)S(1)} %bitcast.24, s32[256]{0:T(256)S(1)} %get-tuple-element.2), kind=kCustom, calls=%fused_computation | custom fusion | bytes 5120 | tf_op jit(solution)/shard_map/scatter | solution.py:44
  20.5 0.7 copy.15
  21.2 16.6 %all-to-all-start = ((s32[128,1,4]{2,1,0:T(1,128)}), s32[128,1,4]{2,1,0:T(1,128)S(1)}, u32[]{:S(2)}, u32[]{:S(2)}) async-start(s32[128,1,4]{2,1,0:T(1,128)} %copy.15), calls=%async_computation | async-start | bytes 131072 | tf_op jit(solution)/shard_map/all_to_all | solution.py:55
  37.8 0.2 fusion.4
  38.0 15.6 %all_gather.3 = bf16[384,768]{1,0:T(8,128)(2,1)S(1)} all-gather(bf16[96,768]{1,0:T(8,128)(2,1)S(1)} %copy-done.1), channel_id=1, replica_groups=mesh['pts'=128,'lmk'=4] {'lmk'}, dimensions={0}, use_global_device_ids=true | all-gather | bytes 737280 | tf_op jit(solution)/shard_map/all_gather | solution.py:33
  53.6 0.2 fusion.1
  53.8 943.7 %all-reduce.2.cloned.1.call-done = bf16[384,512]{1,0:T(8,128)(2,1)} async-done(((bf16[384,512]{1,0:T(8,128)(2,1)}), bf16[384,512]{1,0:T(8,128)(2,1)}) %all-reduce.2.cloned.1.call-update) | async-done | bytes 393232 | tf_op jit(solution)/shard_map/psum | solution.py:12
  997.5 1.7 convolution_convert_fusion
  999.2 0.9 broadcast_in_dim.10
  1000.1 30.6 %scatter_fusion.1 = bf16[128,4,512]{2,1,0:T(4,128)(2,1)} fusion(bf16[128,4,512]{2,1,0:T(4,128)(2,1)} %broadcast_in_dim.10, s32[256]{0:T(256)S(1)} %bitcast.25, bf16[256,512]{1,0:T(8,128)(2,1)S(1)} %convolution_convert_fusion), kind=kCustom, calls=%fused_computation.1 | custom fusion | bytes 788480 | tf_op jit(solution)/shard_map/scatter | solution.py:51
  1030.7 7.8 all-to-all-start.1
  1038.5 0.5 broadcast.135
  1039.0 0.8 reduce.3
  1039.8 0.1 eq.48
  1040.0 0.6 convert_reduce_fusion
  1040.6 16.3 %all-to-all-done.1 = bf16[128,4,512]{2,1,0:T(4,128)(2,1)S(1)} async-done(((bf16[128,4,512]{2,1,0:T(4,128)(2,1)}), bf16[128,4,512]{2,1,0:T(4,128)(2,1)S(1)}, u32[]{:S(2)}, u32[]{:S(2)}) %all-to-all-start.1) | async-done | bytes 524320 | tf_op jit(solution)/shard_map/all_to_all | solution.py:54
  1056.9 0.1 reshape.67
  1057.0 0.8 convolution_multiply_fusion.1
  (20 shorter events, 0.1 us)
Async XLA Ops:
  7.2 990.3 %all-reduce.2.cloned.1.call-start = ((), (), s32[]{:S(2)}) async-start(), calls=%async_computation.2 | async-start | bytes 786432 | tf_op jit(solution)/shard_map/psum | solution.py:12
  7.9 0.8 copy-start.2
  9.4 28.5 %copy-start = (bf16[256,768]{1,0:T(8,128)(2,1)S(1)}, bf16[256,768]{1,0:T(8,128)(2,1)}, u32[]{:S(2)}) copy-start(bf16[256,768]{1,0:T(8,128)(2,1)} %param.5) | copy-start | bytes 1179652
  20.4 17.6 %copy-start.1 = (bf16[96,768]{1,0:T(8,128)(2,1)S(1)}, bf16[96,768]{1,0:T(8,128)(2,1)}, u32[]{:S(2)}) copy-start(bf16[96,768]{1,0:T(8,128)(2,1)} %param.6) | copy-start | bytes 442372
  21.2 1009.5 %all-to-all-start = ((s32[128,1,4]{2,1,0:T(1,128)}), s32[128,1,4]{2,1,0:T(1,128)S(1)}, u32[]{:S(2)}, u32[]{:S(2)}) async-start(s32[128,1,4]{2,1,0:T(1,128)} %copy.15), calls=%async_computation | async-start | bytes 131072 | tf_op jit(solution)/shard_map/all_to_all | solution.py:55
  1030.7 26.2 %all-to-all-start.1 = ((bf16[128,4,512]{2,1,0:T(4,128)(2,1)}), bf16[128,4,512]{2,1,0:T(4,128)(2,1)S(1)}, u32[]{:S(2)}, u32[]{:S(2)}) async-start(bf16[128,4,512]{2,1,0:T(4,128)(2,1)} %scatter_fusion.1), calls=%async_computation.1 | async-start | bytes 1048576 | tf_op jit(solution)/shard_map/all_to_all | solution.py:54
Sparse Core Ops, SparseCore 0:
  10.9 986.5 all-reduce.1
where the time goes:
time: 1070 us; the launch traced here: 1060 us
  waiting for transfers between devices  960 us (90%)
  local copies, waits for them, and re-layouts  44.2 us (4%)
  starting transfers between devices  24.5 us (2%)
  blocking collectives  15.6 us (1%)
  between operations  14.8 us (1%)
    psum x1, waiting for transfers between devices, spread(): return lax.psum(block, axis)  944 us
    scatter x1, local copies, waits for them, and re-layouts, body(): slots = jnp.zeros((point_groups, capacity, features.shape[1]), jnp.bfloat...  30.6 us
  transfers between devices with their start and end apart: 3, of which 2 were waited for; matrix products, arithmetic and copies ran while one was open for 5% of the time, Pallas kernels for 0%

commit v1 on v0

--- a/solution.py
+++ b/solution.py
@@ -7,9 +7,13 @@
 CLUSTERS = 4096
 
 
+def recast_row_over_axis(frame, link_axis):
+    return jax.lax.all_gather(frame, link_axis).sum(axis=0)
+
+
 def spread(block, axis, holder):
     block = jnp.where(lax.axis_index(axis) == holder, block, jnp.zeros_like(block))
-    return lax.psum(block, axis)
+    return recast_row_over_axis(block, axis)
 
 
 def unit_rows(values_in):

time: 1070 us -> 398 us (0.37)
  waiting for transfers between devices: 960 us -> 273 us
  other arithmetic: 3.06 us -> 19.4 us
    psum x1 -> x0, waiting for transfers between devices: 944 us -> none  [spread(): return lax.psum(block, axis)]
    all_gather x0 -> x1, waiting for transfers between devices: none -> 257 us  [recast_row_over_axis(): return jax.lax.all_gather(frame, link_axis).sum(axis=0)]
    reduce_sum x0 -> x1, other arithmetic: none -> 16.3 us  [recast_row_over_axis(): return jax.lax.all_gather(frame, link_axis).sum(axis=0)]
  transfers between devices with their start and end apart: 3 -> 3, of which waited for: 2 -> 2; matrix products, arithmetic and copies ran while one was open for 5% -> 16% of each run, Pallas kernels for 0% -> 0%
where the time goes in v1:
time: 398 us; the launch traced here: 397 us
  waiting for transfers between devices  273 us (69%)
  local copies, waits for them, and re-layouts  44.2 us (11%)
  starting transfers between devices  29.1 us (7%)
  other arithmetic  19.4 us (5%)
  between operations  14.9 us (4%)
  blocking collectives  14.8 us (4%)
    all_gather x1, waiting for transfers between devices, recast_row_over_axis(): return jax.lax.all_gather(frame, link_axis).sum(axis=0)  257 us
    scatter x1, local copies, waits for them, and re-layouts, body(): slots = jnp.zeros((point_groups, capacity, features.shape[1]), jnp.bfloat...  30.6 us
    all_to_all x1, starting transfers between devices, body(): lax.all_to_all(slot_ids, 'pts', split_axis=0, concat_axis=0, tiled=True)  16.6 us
    all_to_all x1, waiting for transfers between devices, body(): lax.all_to_all(slots, 'pts', split_axis=0, concat_axis=0, tiled=True)  16.3 us
    reduce_sum x1, other arithmetic, recast_row_over_axis(): return jax.lax.all_gather(frame, link_axis).sum(axis=0)  16.3 us
    all_gather x1, blocking collectives, body(): lax.all_gather(landmarks, 'lmk', axis=0, tiled=True)  14.8 us
    all_to_all x1, starting transfers between devices, body(): lax.all_to_all(slots, 'pts', split_axis=0, concat_axis=0, tiled=True)  12.5 us
    scatter x1, local copies, waits for them, and re-layouts, body(): jnp.full((point_groups, capacity), -1, jnp.int32).at[owners, slot_rank]  11.1 us
  transfers between devices with their start and end apart: 3, of which 2 were waited for; matrix products, arithmetic and copies ran while one was open for 16% of the time, Pallas kernels for 0%

profile of v1, /device:TPU:1, one launch (start us, length us, event | category | flops | bytes accessed | tf_op | source)
XLA Modules:
  0.0 397.0 jit_solution(9809884800264629)
XLA Ops:
  7.2 0.0 all-gather.2.cloned.1.call-start
  7.9 0.8 broadcast_select_fusion
  8.7 0.1 copy.13
  8.8 0.2 fusion.15
  9.1 0.2 fusion.16
  9.4 11.1 %scatter_fusion = s32[128,4]{0,1:T(4,128)S(1)} fusion(s32[128,4]{0,1:T(4,128)S(1)} %broadcast_in_dim.8, s32[256]{0:T(256)S(1)} %bitcast.24, s32[256]{0:T(256)S(1)} %get-tuple-element.2), kind=kCustom, calls=%fused_computation | custom fusion | bytes 5120 | tf_op jit(solution)/shard_map/scatter | solution.py:48
  20.5 0.7 copy.15
  21.2 16.6 %all-to-all-start = ((s32[128,1,4]{2,1,0:T(1,128)}), s32[128,1,4]{2,1,0:T(1,128)S(1)}, u32[]{:S(2)}, u32[]{:S(2)}) async-start(s32[128,1,4]{2,1,0:T(1,128)} %copy.15), calls=%async_computation | async-start | bytes 131072 | tf_op jit(solution)/shard_map/all_to_all | solution.py:59
  37.9 0.2 fusion.4
  38.0 14.8 %all_gather.7 = bf16[384,768]{1,0:T(8,128)(2,1)S(1)} all-gather(bf16[96,768]{1,0:T(8,128)(2,1)S(1)} %copy-done.1), channel_id=1, replica_groups=mesh['pts'=128,'lmk'=4] {'lmk'}, dimensions={0}, use_global_device_ids=true | all-gather | bytes 737280 | tf_op jit(solution)/shard_map/all_gather | solution.py:37
  52.8 0.2 fusion.1
  53.0 256.8 %all-gather.2.cloned.1.call-done = bf16[128,384,512]{2,1,0:T(8,128)(2,1)} async-done(((bf16[1,384,512]{2,1,0:T(8,128)(2,1)}), bf16[128,384,512]{2,1,0:T(8,128)(2,1)}) %all-gather.2.cloned.1.call-update) | async-done | bytes 50331664 | tf_op jit(solution)/shard_map/all_gather | solution.py:11
  309.8 16.3 %reduce_sum.51 = bf16[384,512]{1,0:T(8,128)(2,1)S(1)} reduce(bf16[128,384,512]{2,1,0:T(8,128)(2,1)} %all-gather.2.cloned.1.call-done, bf16[]{:T(256)} %constant.49.clone.1), dimensions={0}, to_apply=%region_6.7 | reduce | flops 24969216 | bytes 50724864 | tf_op jit(solution)/shard_map/reduce_sum | solution.py:11
  326.1 0.7 convolution_convert_fusion
  326.8 0.9 broadcast_in_dim.10
  327.8 30.6 %scatter_fusion.1 = bf16[128,4,512]{2,1,0:T(4,128)(2,1)} fusion(bf16[128,4,512]{2,1,0:T(4,128)(2,1)} %broadcast_in_dim.10, s32[256]{0:T(256)S(1)} %bitcast.25, bf16[256,512]{1,0:T(8,128)(2,1)S(1)} %convolution_convert_fusion), kind=kCustom, calls=%fused_computation.1 | custom fusion | bytes 788480 | tf_op jit(solution)/shard_map/scatter | solution.py:55
  358.3 12.5 %all-to-all-start.1 = ((bf16[128,4,512]{2,1,0:T(4,128)(2,1)}), bf16[128,4,512]{2,1,0:T(4,128)(2,1)S(1)}, u32[]{:S(2)}, u32[]{:S(2)}) async-start(bf16[128,4,512]{2,1,0:T(4,128)(2,1)} %scatter_fusion.1), calls=%async_computation.1 | async-start | bytes 1048576 | tf_op jit(solution)/shard_map/all_to_all | solution.py:58
  370.8 0.5 broadcast.133
  371.3 0.8 reduce.4
  372.1 0.1 eq.48
  372.2 0.6 convert_reduce_fusion
  372.9 16.3 %all-to-all-done.1 = bf16[128,4,512]{2,1,0:T(4,128)(2,1)S(1)} async-done(((bf16[128,4,512]{2,1,0:T(4,128)(2,1)}), bf16[128,4,512]{2,1,0:T(4,128)(2,1)S(1)}, u32[]{:S(2)}, u32[]{:S(2)}) %all-to-all-start.1) | async-done | bytes 524320 | tf_op jit(solution)/shard_map/all_to_all | solution.py:58
  389.2 0.1 reshape.64
  389.3 0.8 convolution_multiply_fusion.1
  (21 shorter events, 0.2 us)
Async XLA Ops:
  7.2 1.5 copy-start.2
  7.2 302.6 %all-gather.2.cloned.1.call-start = ((), (), s32[]{:S(2)}) async-start(), calls=%async_computation.2 | async-start | bytes 50724864 | tf_op jit(solution)/shard_map/all_gather | solution.py:11
  9.4 28.5 %copy-start = (bf16[256,768]{1,0:T(8,128)(2,1)S(1)}, bf16[256,768]{1,0:T(8,128)(2,1)}, u32[]{:S(2)}) copy-start(bf16[256,768]{1,0:T(8,128)(2,1)} %param.5) | copy-start | bytes 1179652
  9.4 28.6 %copy-start.1 = (bf16[96,768]{1,0:T(8,128)(2,1)S(1)}, bf16[96,768]{1,0:T(8,128)(2,1)}, u32[]{:S(2)}) copy-start(bf16[96,768]{1,0:T(8,128)(2,1)} %param.6) | copy-start | bytes 442372
  21.2 337.1 %all-to-all-start = ((s32[128,1,4]{2,1,0:T(1,128)}), s32[128,1,4]{2,1,0:T(1,128)S(1)}, u32[]{:S(2)}, u32[]{:S(2)}) async-start(s32[128,1,4]{2,1,0:T(1,128)} %copy.15), calls=%async_computation | async-start | bytes 131072 | tf_op jit(solution)/shard_map/all_to_all | solution.py:59
  358.3 30.8 %all-to-all-start.1 = ((bf16[128,4,512]{2,1,0:T(4,128)(2,1)}), bf16[128,4,512]{2,1,0:T(4,128)(2,1)S(1)}, u32[]{:S(2)}, u32[]{:S(2)}) async-start(bf16[128,4,512]{2,1,0:T(4,128)(2,1)} %scatter_fusion.1), calls=%async_computation.1 | async-start | bytes 1048576 | tf_op jit(solution)/shard_map/all_to_all | solution.py:58
Sparse Core Ops, SparseCore 0:
  10.2 299.5 all-gather.1
